TPU v7x, 256 devices: a whole 4x4x8 slice. The times are simulated.
256 devices in a mesh: chan: 16 (over x, y), win: 16 (over z, core).
Axes of the slice: x: 4, y: 4, z: 8, core: 2. Of those that a mesh axis runs over, the one named last changes fastest.
Arguments:
- traces: float32 [16, 160, 48, 2048], P('win', 'chan'), may hold values from -54 to 54
- pair_blocks: int32 [48, 2], replicated, may hold values from 0 to 159, as said below
- pair_count: int32 [16], replicated, may hold values from 1 to 3, 32 in all
Outputs:
- stacks: float32 [64, 48, 2304], P('win', 'chan')
Inputs may be any that keep to these rules, and one draw needn't show every extreme that they name: `pair_blocks`: the blocks of owner o's slots form a chain c_0, ..., c_3: slot 3 * o + k holds (c_k, c_k+1); c_k lies on index q + k of chan (block c lies on index c // 10) for some q of the owner, and 1 <= c_k+1 - c_k <= 16. `pair_count`: the counts sum to 32.
All inputs are finite; a program needn't handle non-finite values.
Results may differ from a plain program's by a relative error of at most 0.0041.
Values may be sent and summed in bfloat16 or wider, within the bound.
A program may use at most 64 MiB of HBM per device.

v0:
```python
import functools
import math

import jax
import jax.numpy as jnp
from jax import lax
from jax.experimental import pallas as pl
from jax.experimental.pallas import tpu as pltpu
from jax.sharding import PartitionSpec as P

LAGS = 64
P_CAP = 3
EPS = 1e-06
TIERS = ((2, 4), (3, 4), (4, 6))
BF16 = jnp.bfloat16
F32 = jnp.float32
MESH = pl.DeviceIdType.MESH

N_MAX = max(t[0] for t in TIERS)
S_MAX = max(t[1] for t in TIERS)
HERE = 2 * N_MAX
OTHER = HERE + S_MAX
SIDE = OTHER + S_MAX
SOURCE = SIDE + S_MAX
LIVE = SOURCE + P_CAP
CHOICE = LIVE + P_CAP
TRASH = CHOICE + 1
TAB = TRASH + 1


def whiten(signal):
    centred = signal - jnp.mean(signal, axis=-1, keepdims=True)
    power = jnp.mean(centred * centred, axis=-1, keepdims=True)
    return (centred * lax.rsqrt(power + EPS)).astype(BF16)


def fetch_blocks(traces, requests, per_peer, my_index, blocks_here):
    owners = requests.shape[0]
    home_index = requests // blocks_here
    is_local = home_index == my_index
    slot_rank = jnp.cumsum(is_local.astype(jnp.int32), axis=1) - 1
    chosen = is_local[:, :, None] & (
        slot_rank[:, :, None] == jnp.arange(per_peer, dtype=jnp.int32)[None, None, :]
    )
    local_block = jnp.sum(
        jnp.where(chosen, requests[:, :, None] - my_index * blocks_here, 0), axis=1
    ).reshape(-1)
    is_valid = jnp.any(chosen, axis=1).reshape(1, -1, 1, 1)
    owner_ids = jnp.arange(owners, dtype=jnp.int32)
    my_requests = jnp.sum(jnp.where((owner_ids == my_index)[:, None], requests, 0), axis=0)
    my_home = my_requests // blocks_here
    request_total = my_requests.shape[0]
    request_ids = jnp.arange(request_total, dtype=jnp.int32)
    earlier = request_ids[None, :] < request_ids[:, None]
    my_rank = jnp.sum((earlier & (my_home[None, :] == my_home[:, None])).astype(jnp.int32), axis=1)
    position = my_home * per_peer + my_rank
    outgoing = jnp.where(
        is_valid, jnp.take(traces, local_block, axis=1), jnp.zeros((), jnp.float32)
    )
    incoming = lax.all_to_all(outgoing, "chan", split_axis=1, concat_axis=1, tiled=True)
    return whiten(jnp.take(incoming, position, axis=1))


def general_path(traces, pair_blocks, pair_count):
    owners = lax.axis_size("chan")
    my_index = lax.axis_index("chan")
    blocks_here = traces.shape[1]
    channels = traces.shape[2]
    samples = traces.shape[3]
    windows = traces.shape[0] * lax.axis_size("win")
    norm_scale = 1.0 / math.sqrt(samples * windows)
    pair_table = pair_blocks.reshape(owners, P_CAP, 2)
    owner_ids = jnp.arange(owners, dtype=jnp.int32)
    mine_row = owner_ids == my_index
    my_count = jnp.sum(jnp.where(mine_row, pair_count, 0))
    requests = jnp.concatenate([pair_table[:, :, 0], pair_table[:, P_CAP - 1 :, 1]], axis=1)
    live_mask = (jnp.arange(P_CAP, dtype=jnp.int32) < my_count).astype(jnp.float32)
    fetched = fetch_blocks(traces, requests, 1, my_index, blocks_here)
    left_side = jnp.stack([fetched[:, row] for row in range(P_CAP)], axis=1)
    right_side = jnp.stack([fetched[:, row + 1] for row in range(P_CAP)], axis=1)
    half_lags = LAGS // 2
    padded = jnp.pad(right_side, ((0, 0), (0, 0), (0, 0), (half_lags, half_lags)))
    weights = live_mask * norm_scale
    width = 8

    def lag_block(first_lag):
        shifted = jnp.stack(
            [
                lax.dynamic_slice_in_dim(padded, first_lag + offset_lag, samples, axis=3)
                for offset_lag in range(width)
            ],
            axis=2,
        )
        product = jnp.einsum(
            "wpit,wpgjt->gpij", left_side, shifted, preferred_element_type=jnp.float32
        )
        return product.reshape(width, P_CAP, channels * channels) * weights[None, :, None]

    firsts = jnp.arange(LAGS // width, dtype=jnp.int32) * width
    partial = lax.map(lag_block, firsts).reshape(
        lax.axis_size("win"), -1, P_CAP, channels * channels
    )
    return jnp.sum(
        lax.all_to_all(partial, "win", split_axis=0, concat_axis=0, tiled=True), axis=0
    )


def kernel(
    n, S, scale, tab, traces, out,
    raw, abuf, bbuf, ysend, yfirst, yrest, xsend, xrecv, acc, zsend, zrecv, own, fsend, frecv,
    load_sem, ys_sem, yr_sem, xs_sem, xr_sem, zs_sem, zr_sem, fs_sem, fr_sem,
):
    n_chan = lax.axis_size("chan")
    n_z = lax.axis_size("win") // 2
    p = lax.axis_index("chan")
    w = lax.axis_index("win")
    z = w // 2
    c = w % 2
    B, CH, TS = raw.shape
    half = CH // 2
    K = abuf.shape[1]

    loads = [pltpu.make_async_copy(traces.at[0, b], raw.at[b], load_sem.at[b]) for b in range(B)]
    for copy in loads:
        copy.start()

    barrier = pltpu.get_barrier_semaphore()
    for d in range(1, n_chan):
        pl.semaphore_signal(
            barrier, inc=1, device_id={"chan": lax.rem(p + d, n_chan)}, device_id_type=MESH
        )
    for d in range(1, n_z):
        pl.semaphore_signal(
            barrier, inc=1, device_id={"win": lax.rem(z + d, n_z) * 2 + c}, device_id_type=MESH
        )
    pl.semaphore_signal(barrier, inc=1, device_id={"win": z * 2 + 1 - c}, device_id_type=MESH)

    bbuf[:, 4 * CH :, :] = jnp.zeros((2, bbuf.shape[1] - 4 * CH, K), BF16)
    for copy in loads:
        copy.wait()

    def y_copy(side, s):
        dst = yfirst.at[side] if s == 0 else yrest.at[side * (n - 1) + s - 1]
        peer = lax.rem(p + (n_chan - 1 if side == 0 else 1), n_chan)
        return pltpu.make_async_remote_copy(
            src_ref=ysend.at[side, s], dst_ref=dst,
            send_sem=ys_sem.at[side, s], recv_sem=yr_sem.at[side, s],
            device_id={"chan": peer}, device_id_type=MESH,
        )

    def first_copy(side):
        return pltpu.make_async_remote_copy(
            src_ref=ysend.at[side, 0], dst_ref=yfirst.at[side],
            send_sem=ys_sem.at[side, 0], recv_sem=yr_sem.at[side, 0],
            device_id={"chan": lax.rem(p + 1, n_chan)}, device_id_type=MESH,
        )

    for s in range(n):
        for side in range(2):
            block = tab[side * N_MAX + s]
            for g in range(0, CH, 16):
                ysend[side, s, g : g + 16, :] = whiten(raw[block, g : g + 16, :])
            if s == 0 and side == 0:
                pl.semaphore_wait(barrier, n_chan - 1 + n_z)
            y_copy(side, s).start()

    zeros = jnp.zeros((16, K - TS), BF16)
    low = lax.broadcasted_iota(jnp.int32, (half, 128), 1) < 64

    def fold(C, write):
        for zz in range(n_z):
            top = C[zz * CH : zz * CH + half, :]
            bottom = C[zz * CH + half : (zz + 1) * CH, :]
            r0 = pltpu.roll(bottom[:, 0:128], 64, 1)
            r1 = pltpu.roll(bottom[:, 128:256], 64, 1)
            write(zz, 0, top[:, 0:128])
            write(zz, 1, jnp.where(low, top[:, 128:256], r0))
            write(zz, 2, jnp.where(low, r0, r1))

    def dot(index):
        return lax.dot_general(
            abuf[...], bbuf[index], (((1,), (1,)), ((), ())), preferred_element_type=F32
        )

    def x_copy(s):
        return pltpu.make_async_remote_copy(
            src_ref=xsend.at[s], dst_ref=xrecv.at[s],
            send_sem=xs_sem.at[s], recv_sem=xr_sem.at[s],
            device_id={"win": z * 2 + 1 - c}, device_id_type=MESH,
        )

    def z_copy(s, d):
        peer = lax.rem(z + d, n_z)
        return pltpu.make_async_remote_copy(
            src_ref=zsend.at[s, peer], dst_ref=zrecv.at[s, d],
            send_sem=zs_sem.at[s, d], recv_sem=zr_sem.at[s, d],
            device_id={"win": peer * 2 + c}, device_id_type=MESH,
        )

    def f_copy(s, d):
        return pltpu.make_async_remote_copy(
            src_ref=fsend.at[s], dst_ref=frecv.at[d * S + s],
            send_sem=fs_sem.at[s, d], recv_sem=fr_sem.at[s, d],
            device_id={"chan": lax.rem(p + d, n_chan)}, device_id_type=MESH,
        )

    def correlate(s, other_of):
        block = tab[HERE + s]
        for g in range(0, CH, 16):
            mine = whiten(raw[block, g : g + 16, :])
            other, is_left = other_of(g)
            left = jnp.where(is_left, mine, other)
            right = jnp.where(is_left, other, mine)
            left = jnp.concatenate([left, zeros], axis=1)
            right = jnp.concatenate([right, zeros], axis=1)
            for zz in range(n_z):
                row = zz * CH + g
                abuf[row : row + 16, :] = pltpu.roll(left, (8 * zz - 25) % K, 1)
            for u in range(8):
                row = (u % 4) * CH + g
                bbuf[u // 4, row : row + 16, :] = pltpu.roll(right, 7 - u, 1)

        def write_send(zz, t, value):
            xsend[s, zz, :, t * 128 : (t + 1) * 128] = value.astype(BF16)

        def write_acc(zz, t, value):
            acc[zz, :, t * 128 : (t + 1) * 128] = value

        fold(dot(1 - c), write_send)
        x_copy(s).start()
        fold(dot(c), write_acc)
        x_copy(s).wait_recv()
        for zz in range(n_z):
            zsend[s, zz] = (acc[zz] + xrecv[s, zz].astype(F32)).astype(BF16)
        own[s] = acc[z] + xrecv[s, z].astype(F32)
        for d in range(1, n_z):
            z_copy(s, d).start()

    @pl.loop(0, 2)
    def _(s):
        first_copy(s).wait_recv()
        correlate(s, lambda g: (yfirst[s, g : g + 16, :], s == 0))

    for side in range(2):
        for t in range(1, n):
            y_copy(side, t).wait_recv()

    @pl.loop(2, S)
    def _(s):
        correlate(s, lambda g: (yrest[tab[OTHER + s], g : g + 16, :], tab[SIDE + s] == 1))

    for s in range(S):
        total = own[s]
        for d in range(1, n_z):
            z_copy(s, d).wait_recv()
            total = total + zrecv[s, d].astype(F32)
        total = total.astype(BF16)
        fsend[s] = total
        for d in range(1, n_chan):
            f_copy(s, d).start()
        frecv[s] = total

    for s in range(S):
        for d in range(1, n_chan):
            f_copy(s, d).wait_recv()
    for k in range(P_CAP):
        out[k] = frecv[tab[SOURCE + k]].astype(F32) * (tab[LIVE + k].astype(F32) * scale)

    for s in range(n):
        for side in range(2):
            y_copy(side, s).wait_send()
    for s in range(S):
        x_copy(s).wait_send()
        for d in range(1, n_z):
            z_copy(s, d).wait_send()
        for d in range(1, n_chan):
            f_copy(s, d).wait_send()


def table_kernel(B, n_chan, blocks, pair_count, tab, counts, ranks, lefts):
    p = lax.axis_index("chan")
    for e in range(n_chan + 4):
        counts[e] = 0
        ranks[e] = 0
        lefts[e] = 0
    for t in range(TAB):
        tab[t] = 0
    starts = []
    lives = []
    for o in range(n_chan):
        start = blocks[2 * P_CAP * o] // B
        live = pair_count[o]
        starts.append(start)
        lives.append(live)
        for k in range(P_CAP):
            counts[start + k] = counts[start + k] + (k < live).astype(jnp.int32)
    rights = [0] * len(TIERS)
    fits = [True] * len(TIERS)
    split = [[] for _ in TIERS]
    for e in range(n_chan):
        count = counts[e]
        for t, (n, S) in enumerate(TIERS):
            right = jnp.maximum(rights[t], 1)
            left = jnp.minimum(jnp.minimum(n, count), S - right)
            split[t].append(left)
            fit = jnp.logical_and(jnp.maximum(left, 1) + right <= S, count - left <= n)
            fits[t] = jnp.logical_and(fits[t], fit)
            rights[t] = count - left
    choice = jnp.int32(len(TIERS))
    n, S = jnp.int32(TIERS[-1][0]), jnp.int32(TIERS[-1][1])
    for t in reversed(range(len(TIERS))):
        choice = jnp.where(fits[t], t, choice)
        n = jnp.where(fits[t], TIERS[t][0], n)
        S = jnp.where(fits[t], TIERS[t][1], S)
    for e in range(n_chan):
        left = split[-1][e]
        for t in reversed(range(len(TIERS))):
            left = jnp.where(fits[t], split[t][e], left)
        lefts[e + 1] = left
    tab[CHOICE] = choice
    for o in range(n_chan):
        for k in range(P_CAP):
            edge = starts[o] + k
            live = k < lives[o]
            rank = ranks[edge]
            ranks[edge] = rank + live.astype(jnp.int32)
            left_here = lefts[edge + 1]
            is_left = rank < left_here
            order = jnp.where(is_left, rank, rank - left_here)
            node = jnp.where(is_left, edge, edge + 1)
            rest = jnp.where(is_left, 1, jnp.maximum(lefts[edge + 2], 1)) + order
            slot = jnp.where(order == 0, jnp.where(is_left, 0, 1), rest)
            first = blocks[2 * (P_CAP * o + k)] - edge * B
            second = blocks[2 * (P_CAP * o + k) + 1] - (edge + 1) * B
            here = jnp.where(is_left, first, second)
            there = jnp.where(is_left, second, first)
            sends = jnp.logical_and(live, 2 * edge + 1 - node == p)
            tab[jnp.where(sends, jnp.where(is_left, 0, N_MAX) + order, TRASH)] = there
            works = jnp.logical_and(live, node == p)
            other = jnp.maximum(order - 1, 0) + jnp.where(is_left, 0, n - 1)
            tab[jnp.where(works, HERE + slot, TRASH)] = here
            tab[jnp.where(works, OTHER + slot, TRASH)] = other
            tab[jnp.where(works, SIDE + slot, TRASH)] = is_left.astype(jnp.int32)
            mine = jnp.logical_and(live, p == o)
            away = p - node
            away = jnp.where(away < 0, away + n_chan, away)
            tab[jnp.where(mine, SOURCE + k, TRASH)] = away * S + slot
            tab[jnp.where(mine, LIVE + k, TRASH)] = 1


def fast_path(tier, traces, tab):
    n, S = TIERS[tier]
    n_chan = lax.axis_size("chan")
    n_win = lax.axis_size("win")
    n_z = n_win // 2
    _, B, CH, TS = traces.shape
    K = TS + 128
    half = CH // 2

    dma = pltpu.SemaphoreType.DMA
    result = pl.pallas_call(
        functools.partial(kernel, n, S, 1.0 / math.sqrt(TS * n_win)),
        out_shape=jax.ShapeDtypeStruct((P_CAP, half, 8 * CH), F32),
        in_specs=[
            pl.BlockSpec(memory_space=pltpu.SMEM),
            pl.BlockSpec(memory_space=pl.ANY),
        ],
        out_specs=pl.BlockSpec(memory_space=pltpu.VMEM),
        scratch_shapes=[
            pltpu.VMEM((B, CH, TS), F32),
            pltpu.VMEM((n_z * CH, K), BF16),
            pltpu.VMEM((2, 256, K), BF16),
            pltpu.VMEM((2, n, CH, TS), BF16),
            pltpu.VMEM((2, CH, TS), BF16),
            pltpu.VMEM((2 * (n - 1), CH, TS), BF16),
            pltpu.VMEM((S, n_z, half, 8 * CH), BF16),
            pltpu.VMEM((S, n_z, half, 8 * CH), BF16),
            pltpu.VMEM((n_z, half, 8 * CH), F32),
            pltpu.VMEM((S, n_z, half, 8 * CH), BF16),
            pltpu.VMEM((S, n_z, half, 8 * CH), BF16),
            pltpu.VMEM((S, half, 8 * CH), F32),
            pltpu.VMEM((S, half, 8 * CH), BF16),
            pltpu.VMEM((n_chan * S, half, 8 * CH), BF16),
            dma((B,)),
            dma((2, n)), dma((2, n)),
            dma((S,)), dma((S,)),
            dma((S, n_z)), dma((S, n_z)),
            dma((S, n_chan)), dma((S, n_chan)),
        ],
        compiler_params=pltpu.CompilerParams(collective_id=tier, has_side_effects=True),
        name=f"stack_pairs_{n}_{S}",
    )(tab, traces)
    result = result.reshape(P_CAP, half, 2, 4, CH)
    return jnp.transpose(result, (3, 0, 2, 1, 4)).reshape(4, P_CAP, CH * CH)


def per_device(traces, pair_blocks, pair_count):
    n_chan = lax.axis_size("chan")
    smem = pl.BlockSpec(memory_space=pltpu.SMEM)
    tab = pl.pallas_call(
        functools.partial(table_kernel, traces.shape[1], n_chan),
        out_shape=jax.ShapeDtypeStruct((TAB,), jnp.int32),
        in_specs=[smem, smem],
        out_specs=smem,
        scratch_shapes=[pltpu.SMEM((n_chan + 4,), jnp.int32)] * 3,
        name="pair_tables",
    )(pair_blocks.reshape(-1), pair_count)
    branches = [
        functools.partial(lambda tier, t, tab, pb, pc: fast_path(tier, t, tab), tier)
        for tier in range(len(TIERS))
    ]
    branches.append(lambda t, tab, pb, pc: general_path(t, pb, pc))
    return lax.switch(tab[CHOICE], branches, traces, tab, pair_blocks, pair_count)


def solution(mesh):
    in_specs = (P("win", "chan", None, None), P(), P())
    out_specs = P("win", "chan", None)
    return jax.shard_map(
        per_device, mesh=mesh, in_specs=in_specs, out_specs=out_specs, check_vma=False
    )
```

profile of v0, /device:TPU:1, one launch (start us, length us, event | category | flops | bytes accessed | tf_op | source)
XLA Modules:
  0.0 58.0 jit_solution(15281318106247882166)
XLA Ops:
  0.0 0.8 %copy.52 = s32[48,2]{1,0:T(8,128)S(1)} copy(s32[48,2]{0,1:T(2,128)} %param.10) | data formatting | bytes 768 | tf_op args[1]
  0.8 0.6 %reshape.241.blocks = s32[96]{0:T(128)} reshape(s32[48,2]{1,0:T(8,128)S(1)} %copy.52) | data formatting | bytes 768 | tf_op jit(solution)/shard_map/reshape | solution.py:407
  1.4 2.9 %pair_tables.1 = s32[34]{0:T(128)S(1)} custom-call(s32[96]{0:T(128)} %reshape.241.blocks, s32[16]{0:T(128)} %pair_count.1), custom_call_target="tpu_custom_call" | custom-call | tf_op jit(solution)/shard_map/pair_tables/pallas_call | solution.py:400
  4.3 0.6 %slice.21 = s32[1]{0:T(128)} slice(s32[34]{0:T(128)S(1)} %pair_tables.1), slice={[32:33]} | slice | bytes 8 | tf_op jit(solution)/shard_map/slice | solution.py:413
  5.6 51.8 %conditional.1 = (f32[4,3,2304]{2,0,1:T(4,128)S(1)}) conditional(s32[]{:T(128)} %bitcast.14, (s32[34]{0:T(128)S(1)}, f32[1,10,48,2048]{3,2,1,0:T(8,128)}) %tuple.29, (s32[34]{0:T(128)S(1)}, f32[1,10,48,2048]{3,2,1,0:T(8,128)}) %tuple.29, (s32[34]{0:T(128)S(1)}, f32[1,10,48,2048]{3,2,1,0:T(8,128)}) %tuple.29, ...), branch_computations={%region_0.0_spmd, %region_1.0_spmd, %region_2.0_spmd, %region_3.15... | conditional | flops 234044496 | bytes 85060200 | solution.py:413
  5.8 49.6 %stack_pairs_3_4.1 = f32[3,24,384]{2,1,0:T(8,128)} custom-call(s32[34]{0:T(128)S(1)} %get-tuple-element.105.tab, f32[1,10,48,2048]{3,2,1,0:T(8,128)} %get-tuple-element.106.traces), custom_call_target="tpu_custom_call" | custom-call | tf_op jit(solution)/shard_map/cond/branch_1_fun/stack_pairs_3_4/pallas_call | solution.py:361
  55.3 1.2 %reshape.231 = f32[3,24,2,4,48]{4,3,2,1,0:T(4,128)S(1)} reshape(f32[3,24,384]{2,1,0:T(8,128)} %stack_pairs_3_4.1) | data formatting | bytes 221184 | tf_op jit(solution)/shard_map/cond/branch_1_fun/reshape | solution.py:393
  56.5 0.1 copy.64
  56.6 0.2 reshape.232
  57.3 0.0 copy-start
  57.3 0.6 %copy-done = f32[4,3,2304]{2,0,1:T(4,128)} copy-done((f32[4,3,2304]{2,0,1:T(4,128)}, f32[4,3,2304]{2,0,1:T(4,128)S(1)}, u32[]{:S(2)}) %copy-start) | copy-done | bytes 110616
Async XLA Ops:
  57.3 0.6 %copy-start = (f32[4,3,2304]{2,0,1:T(4,128)}, f32[4,3,2304]{2,0,1:T(4,128)S(1)}, u32[]{:S(2)}) copy-start(f32[4,3,2304]{2,0,1:T(4,128)S(1)} %get-tuple-element.273) | copy-start | bytes 331780
where the time goes:
time: 58.1 us; the launch traced here: 58 us
  Pallas kernels  52.5 us (90%)
  local copies, waits for them, and re-layouts  4.04 us (7%)
  loops' own time  0.75 us (1%)
  between operations  0.68 us (1%)
    pallas_call x1, Pallas kernels, fast_path(): pl.pallas_call(functools.partial(kernel, n, S, 1.0 / math.sqrt(TS * n_win...  49.6 us
    pallas_call x1, Pallas kernels, per_device(): pl.pallas_call(functools.partial(table_kernel, traces.shape[1], n_chan),...  2.91 us
    unnamed x3, local copies, waits for them, and re-layouts  1.4 us
    reshape x2, local copies, waits for them, and re-layouts, fast_path(): result = result.reshape(P_CAP, half, 2, 4, CH)  1.22 us

commit v1 on v0

--- a/solution.py
+++ b/solution.py
@@ -12,6 +12,7 @@
 P_CAP = 3
 EPS = 1e-06
 TIERS = ((2, 4), (3, 4), (4, 6))
+FINISH = {4: ((3, 0),), 6: ((3, 0), (4, 1), (5, 2))}
 BF16 = jnp.bfloat16
 F32 = jnp.float32
 MESH = pl.DeviceIdType.MESH
@@ -20,11 +21,9 @@
 S_MAX = max(t[1] for t in TIERS)
 HERE = 2 * N_MAX
 OTHER = HERE + S_MAX
-SIDE = OTHER + S_MAX
-SOURCE = SIDE + S_MAX
+SOURCE = OTHER + S_MAX
 LIVE = SOURCE + P_CAP
-CHOICE = LIVE + P_CAP
-TRASH = CHOICE + 1
+TRASH = LIVE + P_CAP
 TAB = TRASH + 1
 
 
@@ -107,8 +106,9 @@
 
 def kernel(
     n, S, scale, tab, traces, out,
-    raw, abuf, bbuf, ysend, yfirst, yrest, xsend, xrecv, acc, zsend, zrecv, own, fsend, frecv,
-    load_sem, ys_sem, yr_sem, xs_sem, xr_sem, zs_sem, zr_sem, fs_sem, fr_sem,
+    raw, abuf, bbuf, ysend, mine, other, xsend, xrecv, acc, zsend, zrecv, own, fsend, frecv,
+    load_sem, ys_sem, yr_sem, xs_sem, xr_sem, zs_sem, zr_sem, fs_sem, fr_sem, z_in, chan_in,
+    *yrecv,
 ):
     n_chan = lax.axis_size("chan")
     n_z = lax.axis_size("win") // 2
@@ -125,34 +125,31 @@
         copy.start()
 
     barrier = pltpu.get_barrier_semaphore()
-    for d in range(1, n_chan):
-        pl.semaphore_signal(
-            barrier, inc=1, device_id={"chan": lax.rem(p + d, n_chan)}, device_id_type=MESH
-        )
-    for d in range(1, n_z):
-        pl.semaphore_signal(
-            barrier, inc=1, device_id={"win": lax.rem(z + d, n_z) * 2 + c}, device_id_type=MESH
-        )
-    pl.semaphore_signal(barrier, inc=1, device_id={"win": z * 2 + 1 - c}, device_id_type=MESH)
+    def chan_peer(d):
+        return {"chan": lax.rem(p + d + n_chan, n_chan)}
+
+    def z_peer(d):
+        return {"win": lax.rem(z + d + n_z, n_z) * 2 + c}
+
+    def signal(sem, device):
+        pl.semaphore_signal(sem, inc=1, device_id=device, device_id_type=MESH)
+
+    for d in (-1, 1):
+        signal(barrier, chan_peer(d))
+        signal(barrier, z_peer(d))
+    signal(barrier, {"win": z * 2 + 1 - c})
 
     bbuf[:, 4 * CH :, :] = jnp.zeros((2, bbuf.shape[1] - 4 * CH, K), BF16)
     for copy in loads:
         copy.wait()
 
     def y_copy(side, s):
-        dst = yfirst.at[side] if s == 0 else yrest.at[side * (n - 1) + s - 1]
+        dst = yrecv[s].at[side]
         peer = lax.rem(p + (n_chan - 1 if side == 0 else 1), n_chan)
         return pltpu.make_async_remote_copy(
             src_ref=ysend.at[side, s], dst_ref=dst,
             send_sem=ys_sem.at[side, s], recv_sem=yr_sem.at[side, s],
             device_id={"chan": peer}, device_id_type=MESH,
-        )
-
-    def first_copy(side):
-        return pltpu.make_async_remote_copy(
-            src_ref=ysend.at[side, 0], dst_ref=yfirst.at[side],
-            send_sem=ys_sem.at[side, 0], recv_sem=yr_sem.at[side, 0],
-            device_id={"chan": lax.rem(p + 1, n_chan)}, device_id_type=MESH,
         )
 
     for s in range(n):
@@ -161,8 +158,23 @@
             for g in range(0, CH, 16):
                 ysend[side, s, g : g + 16, :] = whiten(raw[block, g : g + 16, :])
             if s == 0 and side == 0:
-                pl.semaphore_wait(barrier, n_chan - 1 + n_z)
+                pl.semaphore_wait(barrier, 5)
             y_copy(side, s).start()
+            if s == 0 and side == 1:
+                for d in (-1, 1):
+                    signal(z_in.at[0], z_peer(d))
+                    signal(chan_in.at[0], chan_peer(d))
+            if s == n - 1 and side == 1:
+                pl.semaphore_wait(z_in.at[0], 2)
+                pl.semaphore_wait(chan_in.at[0], 2)
+                for d in (-2, 2):
+                    signal(z_in.at[1], z_peer(d))
+                    signal(chan_in.at[1], chan_peer(d))
+
+    for s in range(S):
+        block = tab[HERE + s]
+        for g in range(0, CH, 16):
+            mine[s, g : g + 16, :] = whiten(raw[block, g : g + 16, :])
 
     zeros = jnp.zeros((16, K - TS), BF16)
     low = lax.broadcasted_iota(jnp.int32, (half, 128), 1) < 64
@@ -204,52 +216,9 @@
             device_id={"chan": lax.rem(p + d, n_chan)}, device_id_type=MESH,
         )
 
-    def correlate(s, other_of):
-        block = tab[HERE + s]
-        for g in range(0, CH, 16):
-            mine = whiten(raw[block, g : g + 16, :])
-            other, is_left = other_of(g)
-            left = jnp.where(is_left, mine, other)
-            right = jnp.where(is_left, other, mine)
-            left = jnp.concatenate([left, zeros], axis=1)
-            right = jnp.concatenate([right, zeros], axis=1)
-            for zz in range(n_z):
-                row = zz * CH + g
-                abuf[row : row + 16, :] = pltpu.roll(left, (8 * zz - 25) % K, 1)
-            for u in range(8):
-                row = (u % 4) * CH + g
-                bbuf[u // 4, row : row + 16, :] = pltpu.roll(right, 7 - u, 1)
-
-        def write_send(zz, t, value):
-            xsend[s, zz, :, t * 128 : (t + 1) * 128] = value.astype(BF16)
-
-        def write_acc(zz, t, value):
-            acc[zz, :, t * 128 : (t + 1) * 128] = value
-
-        fold(dot(1 - c), write_send)
-        x_copy(s).start()
-        fold(dot(c), write_acc)
-        x_copy(s).wait_recv()
-        for zz in range(n_z):
-            zsend[s, zz] = (acc[zz] + xrecv[s, zz].astype(F32)).astype(BF16)
-        own[s] = acc[z] + xrecv[s, z].astype(F32)
-        for d in range(1, n_z):
-            z_copy(s, d).start()
-
-    @pl.loop(0, 2)
-    def _(s):
-        first_copy(s).wait_recv()
-        correlate(s, lambda g: (yfirst[s, g : g + 16, :], s == 0))
-
-    for side in range(2):
-        for t in range(1, n):
-            y_copy(side, t).wait_recv()
-
-    @pl.loop(2, S)
-    def _(s):
-        correlate(s, lambda g: (yrest[tab[OTHER + s], g : g + 16, :], tab[SIDE + s] == 1))
-
-    for s in range(S):
+    def finish(s):
+        if s == 0:
+            pl.semaphore_wait(chan_in.at[2], 2)
         total = own[s]
         for d in range(1, n_z):
             z_copy(s, d).wait_recv()
@@ -260,11 +229,81 @@
             f_copy(s, d).start()
         frecv[s] = total
 
+    @pl.loop(0, S)
+    def _(s):
+        for side in range(2):
+
+            @pl.when(s == side)
+            def _():
+                y_copy(side, 0).wait_recv()
+                other[...] = yrecv[0][side]
+
+        for t in range(1, n):
+
+            @pl.when(s == t + 1)
+            def _():
+                for side in range(2):
+                    y_copy(side, t).wait_recv()
+
+            @pl.when(s == t + 1 if t < n - 1 else s > t)
+            def _():
+                order = tab[OTHER + s] // 2
+                side = 1 - tab[OTHER + s] % 2
+                for g in range(0, CH, 16):
+                    value = yrecv[1][side, g : g + 16, :]
+                    for u in range(2, t + 1):
+                        value = jnp.where(order == u, yrecv[u][side, g : g + 16, :], value)
+                    other[g : g + 16, :] = value
+
+        for late, early in FINISH[S]:
+
+            @pl.when(s == late)
+            def _():
+                finish(early)
+
+        is_left = jnp.where(s < 2, 1 - s, tab[OTHER + s] % 2) == 1
+        for g in range(0, CH, 16):
+            ours = mine[s, g : g + 16, :]
+            theirs = other[g : g + 16, :]
+            left = jnp.where(is_left, ours, theirs)
+            right = jnp.where(is_left, theirs, ours)
+            left = jnp.concatenate([left, zeros], axis=1)
+            right = jnp.concatenate([right, zeros], axis=1)
+            for zz in range(n_z):
+                row = zz * CH + g
+                abuf[row : row + 16, :] = pltpu.roll(left, (8 * zz - 25) % K, 1)
+            for u in range(8):
+                row = (u % 4) * CH + g
+                bbuf[u // 4, row : row + 16, :] = pltpu.roll(right, 7 - u, 1)
+
+        def write_send(zz, t, value):
+            xsend[s, zz, :, t * 128 : (t + 1) * 128] = value.astype(BF16)
+
+        def write_acc(zz, t, value):
+            acc[zz, :, t * 128 : (t + 1) * 128] = value
+
+        fold(dot(1 - c), write_send)
+        x_copy(s).start()
+        fold(dot(c), write_acc)
+        x_copy(s).wait_recv()
+        for zz in range(n_z):
+            zsend[s, zz] = (acc[zz] + xrecv[s, zz].astype(F32)).astype(BF16)
+        own[s] = acc[z] + xrecv[s, z].astype(F32)
+
+        @pl.when(s == 0)
+        def _():
+            pl.semaphore_wait(z_in.at[1], 2)
+            pl.semaphore_wait(chan_in.at[1], 2)
+            for d in (-4, 4):
+                signal(chan_in.at[2], chan_peer(d))
+
+        for d in range(1, n_z):
+            z_copy(s, d).start()
+
+    done = [early for _, early in FINISH[S]]
     for s in range(S):
-        for d in range(1, n_chan):
-            f_copy(s, d).wait_recv()
-    for k in range(P_CAP):
-        out[k] = frecv[tab[SOURCE + k]].astype(F32) * (tab[LIVE + k].astype(F32) * scale)
+        if s not in done:
+            finish(s)
 
     for s in range(n):
         for side in range(2):
@@ -275,30 +314,31 @@
             z_copy(s, d).wait_send()
         for d in range(1, n_chan):
             f_copy(s, d).wait_send()
-
-
-def table_kernel(B, n_chan, blocks, pair_count, tab, counts, ranks, lefts):
+    for s in range(S):
+        for d in range(1, n_chan):
+            f_copy(s, d).wait_recv()
+    for k in range(P_CAP):
+        out[k] = frecv[tab[SOURCE + k]].astype(F32) * (tab[LIVE + k].astype(F32) * scale)
+
+
+def table_kernel(B, n_chan, blocks, pair_count, tab, tier, counts, lefts):
     p = lax.axis_index("chan")
     for e in range(n_chan + 4):
         counts[e] = 0
-        ranks[e] = 0
         lefts[e] = 0
     for t in range(TAB):
         tab[t] = 0
-    starts = []
-    lives = []
-    for o in range(n_chan):
-        start = blocks[2 * P_CAP * o] // B
-        live = pair_count[o]
-        starts.append(start)
-        lives.append(live)
-        for k in range(P_CAP):
-            counts[start + k] = counts[start + k] + (k < live).astype(jnp.int32)
+    starts = [blocks[0, P_CAP * o] // B for o in range(n_chan)]
+    lives = [pair_count[o] for o in range(n_chan)]
+    for start, live in zip(starts, lives):
+        counts[start] = counts[start] + 1
+        counts[start + live] = counts[start + live] - 1
     rights = [0] * len(TIERS)
     fits = [True] * len(TIERS)
     split = [[] for _ in TIERS]
+    count = 0
     for e in range(n_chan):
-        count = counts[e]
+        count = count + counts[e]
         for t, (n, S) in enumerate(TIERS):
             right = jnp.maximum(rights[t], 1)
             left = jnp.minimum(jnp.minimum(n, count), S - right)
@@ -307,45 +347,58 @@
             fits[t] = jnp.logical_and(fits[t], fit)
             rights[t] = count - left
     choice = jnp.int32(len(TIERS))
-    n, S = jnp.int32(TIERS[-1][0]), jnp.int32(TIERS[-1][1])
+    S = jnp.int32(TIERS[-1][1])
     for t in reversed(range(len(TIERS))):
         choice = jnp.where(fits[t], t, choice)
-        n = jnp.where(fits[t], TIERS[t][0], n)
         S = jnp.where(fits[t], TIERS[t][1], S)
     for e in range(n_chan):
         left = split[-1][e]
         for t in reversed(range(len(TIERS))):
             left = jnp.where(fits[t], split[t][e], left)
         lefts[e + 1] = left
-    tab[CHOICE] = choice
-    for o in range(n_chan):
-        for k in range(P_CAP):
-            edge = starts[o] + k
-            live = k < lives[o]
-            rank = ranks[edge]
-            ranks[edge] = rank + live.astype(jnp.int32)
-            left_here = lefts[edge + 1]
-            is_left = rank < left_here
-            order = jnp.where(is_left, rank, rank - left_here)
-            node = jnp.where(is_left, edge, edge + 1)
-            rest = jnp.where(is_left, 1, jnp.maximum(lefts[edge + 2], 1)) + order
-            slot = jnp.where(order == 0, jnp.where(is_left, 0, 1), rest)
-            first = blocks[2 * (P_CAP * o + k)] - edge * B
-            second = blocks[2 * (P_CAP * o + k) + 1] - (edge + 1) * B
-            here = jnp.where(is_left, first, second)
-            there = jnp.where(is_left, second, first)
-            sends = jnp.logical_and(live, 2 * edge + 1 - node == p)
-            tab[jnp.where(sends, jnp.where(is_left, 0, N_MAX) + order, TRASH)] = there
-            works = jnp.logical_and(live, node == p)
-            other = jnp.maximum(order - 1, 0) + jnp.where(is_left, 0, n - 1)
-            tab[jnp.where(works, HERE + slot, TRASH)] = here
-            tab[jnp.where(works, OTHER + slot, TRASH)] = other
-            tab[jnp.where(works, SIDE + slot, TRASH)] = is_left.astype(jnp.int32)
-            mine = jnp.logical_and(live, p == o)
-            away = p - node
-            away = jnp.where(away < 0, away + n_chan, away)
-            tab[jnp.where(mine, SOURCE + k, TRASH)] = away * S + slot
-            tab[jnp.where(mine, LIVE + k, TRASH)] = 1
+    tier[0] = choice
+
+    ranks = [0, 0]
+    left_of = [lefts[p], lefts[p + 1]]
+    rest_of_right = jnp.maximum(left_of[1], 1)
+    for o, (start, live) in enumerate(zip(starts, lives)):
+        for end in range(2):
+            k = p - 1 + end - start
+            here = jnp.logical_and(k >= 0, k < live)
+            row = P_CAP * o + jnp.minimum(jnp.maximum(k, 0), P_CAP - 1)
+            block = blocks[1 - end, row] - p * B
+            rank = ranks[end]
+            ranks[end] = rank + here.astype(jnp.int32)
+            is_left = rank < left_of[end]
+            order = jnp.where(is_left, rank, rank - left_of[end])
+            if end == 0:
+                works = jnp.logical_not(is_left)
+                slot = jnp.where(order == 0, 1, rest_of_right + order)
+            else:
+                works = is_left
+                slot = jnp.where(order == 0, 0, 1 + order)
+            place = jnp.where(works, HERE + slot, end * N_MAX + order)
+            tab[jnp.where(here, place, TRASH)] = block
+            tab[jnp.where(jnp.logical_and(here, works), OTHER + slot, TRASH)] = 2 * order + end
+
+    own_start = blocks[0, P_CAP * p] // B
+    own_live = pair_count[p]
+    for k in range(P_CAP):
+        edge = own_start + k
+        rank = 0
+        for o, (start, live) in enumerate(zip(starts, lives)):
+            inside = jnp.logical_and(edge >= start, edge < start + live)
+            rank = rank + jnp.logical_and(inside, o < p).astype(jnp.int32)
+        left = lefts[edge + 1]
+        is_left = rank < left
+        order = jnp.where(is_left, rank, rank - left)
+        rest = jnp.where(is_left, 1, jnp.maximum(lefts[edge + 2], 1)) + order
+        slot = jnp.where(order == 0, jnp.where(is_left, 0, 1), rest)
+        away = p - jnp.where(is_left, edge, edge + 1)
+        away = jnp.where(away < 0, away + n_chan, away)
+        live = k < own_live
+        tab[SOURCE + k] = jnp.where(live, away * S + slot, 0)
+        tab[LIVE + k] = live.astype(jnp.int32)
 
 
 def fast_path(tier, traces, tab):
@@ -371,8 +424,8 @@
             pltpu.VMEM((n_z * CH, K), BF16),
             pltpu.VMEM((2, 256, K), BF16),
             pltpu.VMEM((2, n, CH, TS), BF16),
-            pltpu.VMEM((2, CH, TS), BF16),
-            pltpu.VMEM((2 * (n - 1), CH, TS), BF16),
+            pltpu.VMEM((S, CH, TS), BF16),
+            pltpu.VMEM((CH, TS), BF16),
             pltpu.VMEM((S, n_z, half, 8 * CH), BF16),
             pltpu.VMEM((S, n_z, half, 8 * CH), BF16),
             pltpu.VMEM((n_z, half, 8 * CH), F32),
@@ -386,7 +439,9 @@
             dma((S,)), dma((S,)),
             dma((S, n_z)), dma((S, n_z)),
             dma((S, n_chan)), dma((S, n_chan)),
-        ],
+            pltpu.SemaphoreType.REGULAR((2,)), pltpu.SemaphoreType.REGULAR((3,)),
+        ]
+        + [pltpu.VMEM((2, CH, TS), BF16)] * n,
         compiler_params=pltpu.CompilerParams(collective_id=tier, has_side_effects=True),
         name=f"stack_pairs_{n}_{S}",
     )(tab, traces)
@@ -397,20 +452,20 @@
 def per_device(traces, pair_blocks, pair_count):
     n_chan = lax.axis_size("chan")
     smem = pl.BlockSpec(memory_space=pltpu.SMEM)
-    tab = pl.pallas_call(
+    tab, tier = pl.pallas_call(
         functools.partial(table_kernel, traces.shape[1], n_chan),
-        out_shape=jax.ShapeDtypeStruct((TAB,), jnp.int32),
+        out_shape=(jax.ShapeDtypeStruct((TAB,), jnp.int32), jax.ShapeDtypeStruct((1,), jnp.int32)),
         in_specs=[smem, smem],
-        out_specs=smem,
-        scratch_shapes=[pltpu.SMEM((n_chan + 4,), jnp.int32)] * 3,
+        out_specs=(smem, smem),
+        scratch_shapes=[pltpu.SMEM((n_chan + 4,), jnp.int32)] * 2,
         name="pair_tables",
-    )(pair_blocks.reshape(-1), pair_count)
+    )(pair_blocks.T, pair_count)
     branches = [
         functools.partial(lambda tier, t, tab, pb, pc: fast_path(tier, t, tab), tier)
         for tier in range(len(TIERS))
     ]
     branches.append(lambda t, tab, pb, pc: general_path(t, pb, pc))
-    return lax.switch(tab[CHOICE], branches, traces, tab, pair_blocks, pair_count)
+    return lax.switch(tier.reshape(()), branches, traces, tab, pair_blocks, pair_count)
 
 
 def solution(mesh):

time: 58.1 us -> 51.5 us (0.89)
  Pallas kernels: 52.5 us -> 48 us
  local copies, waits for them, and re-layouts: 4.04 us -> 2.06 us
    pallas_call x1, Pallas kernels: 49.6 us -> 45.7 us  [fast_path(): pl.pallas_call(functools.partial(kernel, n, S, 1.0 / math.sqrt(TS * n_win...]
    unnamed x3 -> x2, local copies, waits for them, and re-layouts: 1.4 us -> 0.64 us
    pallas_call x1, Pallas kernels: 2.91 us -> 2.25 us  [per_device(): pl.pallas_call(functools.partial(table_kernel, traces.shape[1], n_chan),...]
    reshape x1 -> x0, local copies, waits for them, and re-layouts: 0.64 us -> none  [per_device(): pair_blocks.reshape(-1)]
    slice x1 -> x0, local copies, waits for them, and re-layouts: 0.58 us -> none  [per_device(): tab[CHOICE]]
where the time goes in v1:
time: 51.5 us; the launch traced here: 51 us
  Pallas kernels  48 us (93%)
  local copies, waits for them, and re-layouts  2.06 us (4%)
  between operations  0.67 us (1%)
    pallas_call x1, Pallas kernels, fast_path(): pl.pallas_call(functools.partial(kernel, n, S, 1.0 / math.sqrt(TS * n_win...  45.7 us
    pallas_call x1, Pallas kernels, per_device(): pl.pallas_call(functools.partial(table_kernel, traces.shape[1], n_chan),...  2.25 us
    reshape x2, local copies, waits for them, and re-layouts, fast_path(): result = result.reshape(P_CAP, half, 2, 4, CH)  1.22 us

profile of v1, /device:TPU:1, one launch (start us, length us, event | category | flops | bytes accessed | tf_op | source)
XLA Modules:
  0.0 51.0 jit_solution(13424623950946120118)
XLA Ops:
  0.0 2.3 %pair_tables.1 = (s32[27]{0:T(128)S(1)}, s32[1]{0:T(128)}) custom-call(s32[2,48]{1,0:T(2,128)} %bitcast.137, s32[16]{0:T(128)} %pair_count.1), custom_call_target="tpu_custom_call" | custom-call | tf_op jit(solution)/shard_map/pair_tables/pallas_call | solution.py:455
  2.9 47.4 %conditional.1 = (f32[4,3,2304]{2,0,1:T(4,128)S(1)}) conditional(s32[]{:T(128)} %bitcast.15, (s32[27]{0:T(128)S(1)}, f32[1,10,48,2048]{3,2,1,0:T(8,128)}) %tuple.29, (s32[27]{0:T(128)S(1)}, f32[1,10,48,2048]{3,2,1,0:T(8,128)}) %tuple.29, (s32[27]{0:T(128)S(1)}, f32[1,10,48,2048]{3,2,1,0:T(8,128)}) %tuple.29, ...), branch_computations={%region_0.0_spmd, %region_1.0_spmd, %region_2.0_spmd, %region_3.15... | conditional | flops 234044496 | bytes 85060200 | solution.py:468
  2.9 45.7 %stack_pairs_2_4.1 = f32[3,24,384]{2,1,0:T(8,128)} custom-call(s32[27]{0:T(128)S(1)} %get-tuple-element.103.tab, f32[1,10,48,2048]{3,2,1,0:T(8,128)} %get-tuple-element.104.traces), custom_call_target="tpu_custom_call" | custom-call | tf_op jit(solution)/shard_map/cond/branch_0_fun/stack_pairs_2_4/pallas_call | solution.py:414
  48.6 1.2 %reshape.228 = f32[3,24,2,4,48]{4,3,2,1,0:T(4,128)S(1)} reshape(f32[3,24,384]{2,1,0:T(8,128)} %stack_pairs_2_4.1) | data formatting | bytes 221184 | tf_op jit(solution)/shard_map/cond/branch_0_fun/reshape | solution.py:448
  49.8 0.1 copy.58
  49.9 0.2 reshape.229
  50.3 0.0 copy-start
  50.3 0.6 %copy-done = f32[4,3,2304]{2,0,1:T(4,128)} copy-done((f32[4,3,2304]{2,0,1:T(4,128)}, f32[4,3,2304]{2,0,1:T(4,128)S(1)}, u32[]{:S(2)}) %copy-start) | copy-done | bytes 110616
Async XLA Ops:
  50.3 0.6 %copy-start = (f32[4,3,2304]{2,0,1:T(4,128)}, f32[4,3,2304]{2,0,1:T(4,128)S(1)}, u32[]{:S(2)}) copy-start(f32[4,3,2304]{2,0,1:T(4,128)S(1)} %get-tuple-element.277) | copy-start | bytes 331780

commit v2 on v1

--- a/solution.py
+++ b/solution.py
@@ -11,8 +11,9 @@
 LAGS = 64
 P_CAP = 3
 EPS = 1e-06
-TIERS = ((2, 4), (3, 4), (4, 6))
-FINISH = {4: ((3, 0),), 6: ((3, 0), (4, 1), (5, 2))}
+TIERS = ((2, 3), (3, 4), (4, 5), (4, 6))
+DIRECT = (4, 3, 5, 2, 6, 1, 7)
+FINISH = {3: (), 4: (), 5: ((4, 0),), 6: ((4, 0), (5, 1))}
 BF16 = jnp.bfloat16
 F32 = jnp.float32
 MESH = pl.DeviceIdType.MESH
@@ -120,10 +121,6 @@
     half = CH // 2
     K = abuf.shape[1]
 
-    loads = [pltpu.make_async_copy(traces.at[0, b], raw.at[b], load_sem.at[b]) for b in range(B)]
-    for copy in loads:
-        copy.start()
-
     barrier = pltpu.get_barrier_semaphore()
     def chan_peer(d):
         return {"chan": lax.rem(p + d + n_chan, n_chan)}
@@ -139,7 +136,12 @@
         signal(barrier, z_peer(d))
     signal(barrier, {"win": z * 2 + 1 - c})
 
-    bbuf[:, 4 * CH :, :] = jnp.zeros((2, bbuf.shape[1] - 4 * CH, K), BF16)
+    loads = [pltpu.make_async_copy(traces.at[0, b], raw.at[b], load_sem.at[b]) for b in range(B)]
+    for copy in loads:
+        copy.start()
+
+    for h in range(2):
+        bbuf[256 * h + 4 * CH : 256 * (h + 1), :] = jnp.zeros((256 - 4 * CH, K), BF16)
     for copy in loads:
         copy.wait()
 
@@ -189,9 +191,9 @@
             write(zz, 1, jnp.where(low, top[:, 128:256], r0))
             write(zz, 2, jnp.where(low, r0, r1))
 
-    def dot(index):
+    def dot():
         return lax.dot_general(
-            abuf[...], bbuf[index], (((1,), (1,)), ((), ())), preferred_element_type=F32
+            abuf[...], bbuf[...], (((1,), (1,)), ((), ())), preferred_element_type=F32
         )
 
     def x_copy(s):
@@ -216,11 +218,24 @@
             device_id={"chan": lax.rem(p + d, n_chan)}, device_id_type=MESH,
         )
 
+    def join(s):
+        x_copy(s).wait_recv()
+        for zz in range(n_z):
+            zsend[s, zz] = (acc[zz] + xrecv[s, zz].astype(F32)).astype(BF16)
+        own[s] = acc[z] + xrecv[s, z].astype(F32)
+
+        @pl.when(s == 0)
+        def _():
+            pl.semaphore_wait(z_in.at[1], 2)
+
+        for d in DIRECT:
+            z_copy(s, d).start()
+
     def finish(s):
         if s == 0:
             pl.semaphore_wait(chan_in.at[2], 2)
         total = own[s]
-        for d in range(1, n_z):
+        for d in DIRECT:
             z_copy(s, d).wait_recv()
             total = total + zrecv[s, d].astype(F32)
         total = total.astype(BF16)
@@ -271,10 +286,10 @@
             right = jnp.concatenate([right, zeros], axis=1)
             for zz in range(n_z):
                 row = zz * CH + g
-                abuf[row : row + 16, :] = pltpu.roll(left, (8 * zz - 25) % K, 1)
+                abuf[row : row + 16, :] = pltpu.roll(left, (8 * zz - 32) % K, 1)
             for u in range(8):
-                row = (u % 4) * CH + g
-                bbuf[u // 4, row : row + 16, :] = pltpu.roll(right, 7 - u, 1)
+                at = pl.multiple_of((1 - c if u < 4 else c) * 256, 256)
+                bbuf[pl.ds(at + (u % 4) * CH + g, 16), :] = pltpu.roll(right, (-u) % K, 1)
 
         def write_send(zz, t, value):
             xsend[s, zz, :, t * 128 : (t + 1) * 128] = value.astype(BF16)
@@ -282,23 +297,19 @@
         def write_acc(zz, t, value):
             acc[zz, :, t * 128 : (t + 1) * 128] = value
 
-        fold(dot(1 - c), write_send)
+        both = dot()
+        theirs_half, ours_half = both[:, :256], both[:, 256:]
+        fold(theirs_half, write_send)
         x_copy(s).start()
-        fold(dot(c), write_acc)
-        x_copy(s).wait_recv()
-        for zz in range(n_z):
-            zsend[s, zz] = (acc[zz] + xrecv[s, zz].astype(F32)).astype(BF16)
-        own[s] = acc[z] + xrecv[s, z].astype(F32)
 
         @pl.when(s == 0)
         def _():
-            pl.semaphore_wait(z_in.at[1], 2)
             pl.semaphore_wait(chan_in.at[1], 2)
             for d in (-4, 4):
                 signal(chan_in.at[2], chan_peer(d))
 
-        for d in range(1, n_z):
-            z_copy(s, d).start()
+        fold(ours_half, write_acc)
+        join(s)
 
     done = [early for _, early in FINISH[S]]
     for s in range(S):
@@ -310,7 +321,7 @@
             y_copy(side, s).wait_send()
     for s in range(S):
         x_copy(s).wait_send()
-        for d in range(1, n_z):
+        for d in DIRECT:
             z_copy(s, d).wait_send()
         for d in range(1, n_chan):
             f_copy(s, d).wait_send()
@@ -422,7 +433,7 @@
         scratch_shapes=[
             pltpu.VMEM((B, CH, TS), F32),
             pltpu.VMEM((n_z * CH, K), BF16),
-            pltpu.VMEM((2, 256, K), BF16),
+            pltpu.VMEM((512, K), BF16),
             pltpu.VMEM((2, n, CH, TS), BF16),
             pltpu.VMEM((S, CH, TS), BF16),
             pltpu.VMEM((CH, TS), BF16),

time: 51.5 us -> 50.6 us (0.983)
  Pallas kernels: 48 us -> 47.4 us
    pallas_call x1, Pallas kernels: 45.7 us -> 45.1 us  [fast_path(): pl.pallas_call(functools.partial(kernel, n, S, 1.0 / math.sqrt(TS * n_win...]
where the time goes in v2:
time: 50.6 us; the launch traced here: 50.4 us
  Pallas kernels  47.4 us (94%)
  local copies, waits for them, and re-layouts  2.06 us (4%)
  between operations  0.67 us (1%)
    pallas_call x1, Pallas kernels, fast_path(): pl.pallas_call(functools.partial(kernel, n, S, 1.0 / math.sqrt(TS * n_win...  45.1 us
    pallas_call x1, Pallas kernels, per_device(): pl.pallas_call(functools.partial(table_kernel, traces.shape[1], n_chan),...  2.35 us
    reshape x2, local copies, waits for them, and re-layouts, fast_path(): result = result.reshape(P_CAP, half, 2, 4, CH)  1.22 us

profile of v2, /device:TPU:1, one launch (start us, length us, event | category | flops | bytes accessed | tf_op | source)
XLA Modules:
  0.0 50.4 jit_solution(10782749482362500810)
XLA Ops:
  0.0 2.3 %pair_tables.1 = (s32[27]{0:T(128)S(1)}, s32[1]{0:T(128)}) custom-call(s32[2,48]{1,0:T(2,128)} %bitcast.145, s32[16]{0:T(128)} %pair_count.1), custom_call_target="tpu_custom_call" | custom-call | tf_op jit(solution)/shard_map/pair_tables/pallas_call | solution.py:466
  3.0 46.8 %conditional.1 = (f32[4,3,2304]{2,0,1:T(4,128)S(1)}) conditional(s32[]{:T(128)} %bitcast.16, (s32[27]{0:T(128)S(1)}, f32[1,10,48,2048]{3,2,1,0:T(8,128)}) %tuple.32, (s32[27]{0:T(128)S(1)}, f32[1,10,48,2048]{3,2,1,0:T(8,128)}) %tuple.32, (s32[27]{0:T(128)S(1)}, f32[1,10,48,2048]{3,2,1,0:T(8,128)}) %tuple.32, ...), branch_computations={%region_0.0_spmd, %region_1.0_spmd, %region_2.0_spmd, %region_3.0_... | conditional | flops 234044496 | bytes 85060200 | solution.py:479
  3.0 45.1 %stack_pairs_3_4.1 = f32[3,24,384]{2,1,0:T(8,128)} custom-call(s32[27]{0:T(128)S(1)} %get-tuple-element.110.tab, f32[1,10,48,2048]{3,2,1,0:T(8,128)} %get-tuple-element.111.traces), custom_call_target="tpu_custom_call" | custom-call | tf_op jit(solution)/shard_map/cond/branch_1_fun/stack_pairs_3_4/pallas_call | solution.py:425
  48.1 1.2 %reshape.234 = f32[3,24,2,4,48]{4,3,2,1,0:T(4,128)S(1)} reshape(f32[3,24,384]{2,1,0:T(8,128)} %stack_pairs_3_4.1) | data formatting | bytes 221184 | tf_op jit(solution)/shard_map/cond/branch_1_fun/reshape | solution.py:459
  49.3 0.1 copy.68
  49.4 0.2 reshape.235
  49.8 0.0 copy-start
  49.8 0.6 %copy-done = f32[4,3,2304]{2,0,1:T(4,128)} copy-done((f32[4,3,2304]{2,0,1:T(4,128)}, f32[4,3,2304]{2,0,1:T(4,128)S(1)}, u32[]{:S(2)}) %copy-start) | copy-done | bytes 110616
Async XLA Ops:
  49.8 0.6 %copy-start = (f32[4,3,2304]{2,0,1:T(4,128)}, f32[4,3,2304]{2,0,1:T(4,128)S(1)}, u32[]{:S(2)}) copy-start(f32[4,3,2304]{2,0,1:T(4,128)S(1)} %get-tuple-element.287) | copy-start | bytes 331780
